TPU v7x, 512 devices: a whole 4x8x8 slice. The times are simulated.
512 devices in a mesh: band: 64 (over z_lo, y, core), strip: 8 (over z_hi, x).
Axes of the slice: x: 4, y: 8, z: 8 (z_hi: 2, z_lo: 4; z = z_hi * 4 + z_lo), core: 2. Of those that a mesh axis runs over, the one named last changes fastest.
Arguments:
- activations: bfloat16 [64, 320, 48, 128], P('band', None, 'strip'), may hold values from -16 to 16
- out_grad: bfloat16 [64, 320, 48, 128], P('band', None, 'strip'), may hold values from -6 to 6
- kernel: bfloat16 [320, 9, 320], P('band', None, 'strip'), may hold values from -0.109375 to 0.109375
Outputs:
- input_grad: bfloat16 [64, 320, 48, 128], P('band', None, 'strip')
- kernel_grad: float32 [320, 9, 320], P('band', None, 'strip')
All inputs are finite; a program needn't handle non-finite values.
Results may differ from a plain program's by a relative error of at most 0.001.
Values may be sent and summed in bfloat16 or wider, within the bound.
A program may use at most 64 MiB of HBM per device.

v0:
```python
import math
import jax
import jax.numpy as jnp
from jax import lax
from jax.sharding import PartitionSpec as P

OFFSETS = ((-1, -1), (-1, 0), (-1, 1), (0, -1), (0, 0), (0, 1), (1, -1), (1, 0), (1, 1))


def extended(cells, sides, width):
    for axis, dim in sides:
        count = lax.axis_size(axis)
        ends = count - 1
        head = lax.slice_in_dim(cells, 0, width, axis=dim)
        tail = lax.slice_in_dim(cells, cells.shape[dim] - width, cells.shape[dim], axis=dim)
        cells = jnp.concatenate(
            [
                lax.ppermute(tail, axis, [(i, (i + 1) % count) for i in range(ends)]),
                cells,
                lax.ppermute(head, axis, [((i + 1) % count, i) for i in range(ends)]),
            ],
            axis=dim,
        )
    return cells


def tap_slice(field, row_step, col_step):
    row_count = field.shape[2] - 2
    col_count = field.shape[3] - 2
    return field[
        :, :, 1 + row_step : 1 + row_step + row_count, 1 + col_step : 1 + col_step + col_count
    ]


def body(activations, out_grad, kernel):
    images = activations.shape[0]
    row_count = activations.shape[2]
    col_count = activations.shape[3]
    cell_total = images * lax.axis_size("band") * row_count * lax.axis_size("strip") * col_count
    grad_scale = 1.0 / math.sqrt(cell_total)
    grad_padded = extended(out_grad, (("strip", 2),), 1)
    grad_padded = jnp.pad(grad_padded, ((0, 0), (0, 0), (0, 0), (1, 1)))
    kernel_full_cols = lax.all_gather(kernel, "strip", axis=2, tiled=True)
    kernel_whole = lax.all_gather(kernel_full_cols, "band", axis=0, tiled=True)
    summed = jnp.zeros((images, kernel_whole.shape[0], row_count, col_count), jnp.float32)
    for tap_index, (row_step, col_step) in enumerate(OFFSETS):
        shifted = tap_slice(grad_padded, -row_step, -col_step)
        summed = summed + jnp.einsum(
            "io,bohw->bihw",
            kernel_whole[:, tap_index, :],
            shifted,
            preferred_element_type=jnp.float32,
        )
    input_grad = summed.astype(jnp.bfloat16)
    blocks = []
    for tap_index, (row_step, col_step) in enumerate(OFFSETS):
        grad_side = tap_slice(grad_padded, -row_step, -col_step)
        blocks.append(
            jnp.einsum("bihw,bohw->io", activations, grad_side, preferred_element_type=jnp.float32)
        )
    partial_value = lax.psum_scatter(
        jnp.stack(blocks, axis=1), "band", scatter_dimension=0, tiled=True
    )
    kernel_sum = lax.psum_scatter(partial_value, "strip", scatter_dimension=2, tiled=True)
    return (input_grad, kernel_sum * grad_scale)


def solution(mesh):
    in_specs = (
        P("band", None, "strip", None),
        P("band", None, "strip", None),
        P("band", None, "strip"),
    )
    out_specs = (P("band", None, "strip", None), P("band", None, "strip"))
    return jax.shard_map(body, mesh=mesh, in_specs=in_specs, out_specs=out_specs, check_vma=False)
```

profile of v0, /device:TPU:4, one launch (start us, length us, event | category | flops | bytes accessed | tf_op | source)
XLA Modules:
  0.0 532.6 jit_solution(4342535424170789729)
XLA Ops:
  7.2 0.0 copy-start
  7.2 0.0 all-gather.2.cloned.1.call-start
  7.2 0.9 copy.21
  8.1 0.0 copy-start.1
  8.2 48.1 %all_gather.6 = bf16[5,9,320]{1,0,2:T(8,128)(2,1)S(1)} all-gather(bf16[5,9,40]{1,0,2:T(8,128)(2,1)S(1)} %copy.21), channel_id=1, replica_groups=mesh['band'=64,'strip'=8] {'strip'}, dimensions={2}, use_global_device_ids=true | all-gather | bytes 32400 | tf_op jit(solution)/shard_map/all_gather | solution.py:43
  56.3 1.0 copy.22
  57.3 0.0 all-gather.2.cloned.1.call-update
  57.3 0.0 reduce-scatter.3.cloned.1.call-start
  57.3 0.9 fusion.42
  58.3 3.0 collective-permute-start.1
  61.3 2.8 collective-permute-start
  64.1 0.5 collective-permute-done.1
  64.6 3.3 collective-permute-done
  68.0 1.7 fusion.6
  69.7 0.0 copy-done
  69.7 1.3 fusion.17
  71.0 0.0 copy-done.1
  71.0 1.3 fusion.16
  72.2 1.3 fusion.15
  73.5 1.3 fusion.14
  74.8 1.2 fusion.13
  76.0 1.3 fusion.12
  77.2 1.3 fusion.11
  78.5 1.2 fusion.10
  79.7 1.2 fusion.9
  81.0 9.0 %copy.33 = f32[320,9,320]{2,1,0:T(8,128)} copy(f32[320,9,320]{0,2,1:T(8,128)} %fusion.9) | data formatting | bytes 7372800 | tf_op jit(solution)/shard_map/stack | solution.py:62
  89.9 0.0 reduce-scatter.3.cloned.1.call-update
  90.0 1.3 dynamic-slice
  91.9 87.8 %all-gather.2.cloned.1.call-done = bf16[320,9,320]{2,1,0:T(8,128)(2,1)} async-done(((bf16[5,9,320]{2,1,0:T(8,128)(2,1)}), bf16[320,9,320]{2,1,0:T(8,128)(2,1)}) %all-gather.2.cloned.1.call-update) | async-done | bytes 1843216 | tf_op jit(solution)/shard_map/all_gather | solution.py:44
  179.7 10.5 %fusion.41 = (bf16[320,1,320]{2,1,0:T(2,128)(2,1)S(1)}, bf16[320,1,320]{2,1,0:T(2,128)(2,1)S(1)}, bf16[320,1,320]{2,1,0:T(2,128)(2,1)S(1)}, bf16[320,1,320]{2,1,...) fusion(bf16[320,9,320]{2,1,0:T(8,128)(2,1)} %all-gather.2.clone, ...), kind=kLoop, calls=%fused_computation.73 | loop fusion | bytes 3686400 | tf_op jit(solution)/shard_map/slice | solution.py:50
  190.3 0.4 fusion.32
  190.7 0.5 fusion.31
  191.2 0.4 convolution_add_fusion.6
  191.6 0.4 convolution_add_fusion.5
  192.0 0.5 convolution_add_fusion.4
  192.5 0.4 convolution_add_fusion.3
  193.0 0.4 convolution_add_fusion.2
  193.4 0.5 convolution_add_fusion.1
  193.9 1.2 fusion.8
  195.1 280.4 %reduce-scatter.3.cloned.1.call-done = f32[5,9,320]{2,1,0:T(8,128)} async-done(((f32[320,9,320]{2,1,0:T(8,128)}), f32[5,9,320]{2,1,0:T(8,128)}) %reduce-scatter.3.cloned.1.call-update) | async-done | bytes 57616 | tf_op jit(solution)/shard_map/reduce_scatter | solution.py:61
  475.5 49.6 %all-reduce.1 = f32[5,9,320]{2,1,0:T(8,128)S(1)} all-reduce(f32[5,9,320]{2,1,0:T(8,128)} %reduce-scatter.3.cloned.1.call-done), channel_id=3, replica_groups=mesh['band'=64,'strip'=8] {'strip'}, use_global_device_ids=true, to_apply=%region_1.2.clone | all-reduce | flops 14400 | bytes 115200
  525.1 0.1 dynamic-slice_multiply_fusion
  525.2 0.6 copy.34
Async XLA Ops:
  7.2 62.5 %copy-start = (bf16[1,320,6,128]{3,1,2,0:T(8,128)(2,1)S(1)}, bf16[1,320,6,128]{3,1,2,0:T(8,128)(2,1)}, u32[]{:S(2)}) copy-start(bf16[1,320,6,128]{3,1,2,0:T(8,128)(2,1)} %param.3) | copy-start | bytes 1474564
  7.2 172.5 %all-gather.2.cloned.1.call-start = ((), (), s32[]{:S(2)}) async-start(), calls=%async_computation.1 | async-start | bytes 3993600 | tf_op jit(solution)/shard_map/all_gather | solution.py:44
  8.1 62.8 %copy-start.1 = (bf16[1,320,6,128]{3,1,2,0:T(8,128)(2,1)S(1)}, bf16[1,320,6,128]{3,1,2,0:T(8,128)(2,1)}, u32[]{:S(2)}) copy-start(bf16[1,320,6,128]{3,1,2,0:T(8,128)(2,1)} %param.4) | copy-start | bytes 1474564
  57.3 418.2 %reduce-scatter.3.cloned.1.call-start = ((), (), s32[]{:S(2)}) async-start(), calls=%async_computation.2 | async-start | bytes 7987200 | tf_op jit(solution)/shard_map/reduce_scatter | solution.py:61
  58.3 6.3 %collective-permute-start.1 = (bf16[1,320,1,128]{3,1,2,0:T(8,128)(2,1)S(1)}, bf16[1,320,1,128]{3,1,2,0:T(8,128)(2,1)S(1)}, u32[]{:S(2)}, u32[]{:S(2)}) collective-permute-start(bf16[1,320,1,128]{3,1,2,0:T(8,128)(2,1)S(1)} %get-tuple-element.18), channel_id=1, source_target_pairs={{1,0},{2,1},{3,2},{4,3},{5,4},{6,5},{7,6},{9,8},{10,9},{11,10},{12... | collective-permute-start | bytes 245768 | tf_op jit(solution)/shard_map/ppermute | solution.py:20
  61.3 6.6 %collective-permute-start = (bf16[1,320,1,128]{3,1,2,0:T(8,128)(2,1)S(1)}, bf16[1,320,1,128]{3,1,2,0:T(8,128)(2,1)S(1)}, u32[]{:S(2)}, u32[]{:S(2)}) collective-permute-start(bf16[1,320,1,128]{3,1,2,0:T(8,128)(2,1)S(1)} %get-tuple-element.17), channel_id=1, source_target_pairs={{0,1},{1,2},{2,3},{3,4},{4,5},{5,6},{6,7},{8,9},{9,10},{10,11},{11... | collective-permute-start | bytes 245768 | tf_op jit(solution)/shard_map/ppermute | solution.py:18
Sparse Core Ops, SparseCore 0:
  57.4 122.2 all-gather.1
  182.6 292.8 reduce-scatter.2
where the time goes:
time: 533 us
  waiting for transfers between devices  372 us (70%)
  blocking collectives  97.7 us (18%)
  local copies, waits for them, and re-layouts  24.3 us (5%)
  matrix products  16.1 us (3%)
  between operations  14.8 us (3%)
  starting transfers between devices  5.92 us (1%)
    reduce_scatter x1, waiting for transfers between devices, body(): lax.psum_scatter(jnp.stack(blocks, axis=1), 'band', scatter_dimension=0,...  280 us
    all_gather x1, waiting for transfers between devices, body(): kernel_whole = lax.all_gather(kernel_full_cols, 'band', axis=0, tiled=True)  87.8 us
    unnamed x1, blocking collectives  49.6 us
    all_gather x1, blocking collectives, body(): kernel_full_cols = lax.all_gather(kernel, 'strip', axis=2, tiled=True)  48.1 us
    dot_general x9, matrix products, body(): jnp.einsum('bihw,bohw->io', activations, grad_side, preferred_element_typ...  11.3 us
  transfers between devices with their start and end apart: 4, of which 4 were waited for; matrix products, arithmetic and copies ran while one was open for 7% of the time, Pallas kernels for 0%

commit v1 on v0

--- a/solution.py
+++ b/solution.py
@@ -41,7 +41,9 @@
     grad_padded = extended(out_grad, (("strip", 2),), 1)
     grad_padded = jnp.pad(grad_padded, ((0, 0), (0, 0), (0, 0), (1, 1)))
     kernel_full_cols = lax.all_gather(kernel, "strip", axis=2, tiled=True)
-    kernel_whole = lax.all_gather(kernel_full_cols, "band", axis=0, tiled=True)
+    kernel_whole = jnp.concatenate(
+        lax.all_to_all(jnp.stack([kernel_full_cols] * lax.axis_size("band")), "band", 0, 0), axis=0
+    )
     summed = jnp.zeros((images, kernel_whole.shape[0], row_count, col_count), jnp.float32)
     for tap_index, (row_step, col_step) in enumerate(OFFSETS):
         shifted = tap_slice(grad_padded, -row_step, -col_step)

time: 533 us -> 431 us (0.81)
  the two profiles are of different devices: /device:TPU:4 before, /device:TPU:0 now
where the time goes in v1:
time: 431 us; the launch traced here: 430 us
  waiting for transfers between devices  254 us (59%)
  blocking collectives  102 us (24%)
  local copies, waits for them, and re-layouts  25.2 us (6%)
  matrix products  18.1 us (4%)
  between operations  14.8 us (3%)
  starting transfers between devices  14.3 us (3%)
    reduce_scatter x1, waiting for transfers between devices, body(): lax.psum_scatter(jnp.stack(blocks, axis=1), 'band', scatter_dimension=0,...  159 us
    all_to_all x1, waiting for transfers between devices, body(): lax.all_to_all(jnp.stack([kernel_full_cols] * lax.axis_size('band')), 'ba...  92.2 us
    unnamed x1, blocking collectives  54.7 us
    all_gather x1, blocking collectives, body(): kernel_full_cols = lax.all_gather(kernel, 'strip', axis=2, tiled=True)  47.2 us
    dot_general x9, matrix products, body(): jnp.einsum('bihw,bohw->io', activations, grad_side, preferred_element_typ...  11.3 us
    another operation x1, local copies, waits for them, and re-layouts, body(): jnp.stack(blocks, axis=1)  8.98 us
  transfers between devices with their start and end apart: 4, of which 4 were waited for; matrix products, arithmetic and copies ran while one was open for 5% of the time, Pallas kernels for 0%

profile of v1, /device:TPU:0, one launch (start us, length us, event | category | flops | bytes accessed | tf_op | source)
XLA Modules:
  0.0 429.8 jit_solution(18204757727240311585)
XLA Ops:
  7.2 0.0 copy-start
  7.2 0.0 copy-start.1
  7.2 0.0 reduce-scatter.3.cloned.1.call-start
  7.2 1.0 fusion.41
  8.3 1.3 collective-permute-start.1
  9.6 4.6 %collective-permute-start = (bf16[1,320,1,128]{3,1,2,0:T(8,128)(2,1)S(1)}, bf16[1,320,1,128]{3,1,2,0:T(8,128)(2,1)S(1)}, u32[]{:S(2)}, u32[]{:S(2)}) collective-permute-start(bf16[1,320,1,128]{3,1,2,0:T(8,128)(2,1)S(1)} %get-tuple-element.10), channel_id=1, source_target_pairs={{0,1},{1,2},{2,3},{3,4},{4,5},{5,6},{6,7},{8,9},{9,10},{10,11},{11... | collective-permute-start | bytes 245768 | tf_op jit(solution)/shard_map/ppermute | solution.py:18
  14.1 0.5 collective-permute-done.1
  14.6 1.6 collective-permute-done
  16.1 1.7 fusion.6
  17.8 0.0 copy-done
  17.8 1.3 fusion.17
  19.1 0.0 copy-done.1
  19.1 1.3 fusion.16
  20.4 1.3 fusion.15
  21.7 1.3 fusion.14
  23.0 1.2 fusion.13
  24.2 1.3 fusion.12
  25.4 1.3 fusion.11
  26.7 1.2 fusion.10
  27.9 1.2 fusion.9
  29.1 9.0 %copy.19 = f32[320,9,320]{2,1,0:T(8,128)} copy(f32[320,9,320]{0,2,1:T(8,128)} %fusion.9) | data formatting | bytes 7372800 | tf_op jit(solution)/shard_map/stack | solution.py:64
  38.1 0.0 copy-start.3
  38.1 0.0 reduce-scatter.3.cloned.1.call-update
  38.1 0.7 copy-done.3
  38.8 0.2 copy.15
  39.0 47.2 %all_gather.3 = bf16[5,9,320]{1,0,2:T(8,128)(2,1)S(1)} all-gather(bf16[5,9,40]{1,0,2:T(8,128)(2,1)S(1)} %copy.15), channel_id=1, replica_groups=mesh['band'=64,'strip'=8] {'strip'}, dimensions={2}, use_global_device_ids=true | all-gather | bytes 32400 | tf_op jit(solution)/shard_map/all_gather | solution.py:43
  86.2 0.5 copy.16
  86.7 2.2 stack.22
  88.8 8.5 %all-to-all-start = ((bf16[64,5,9,320]{3,1,2,0:T(8,128)(2,1)}), bf16[64,5,9,320]{3,1,2,0:T(8,128)(2,1)}, u32[]{:S(2)}, u32[]{:S(2)}) async-start(bf16[64,5,9,320]{3,1,2,0:T(8,128)(2,1)} %stack.22), calls=%async_computation | async-start | bytes 7077888 | tf_op jit(solution)/shard_map/all_to_all | solution.py:45
  97.3 1.3 dynamic-slice
  99.2 92.2 %all-to-all-done = bf16[64,5,9,320]{3,1,2,0:T(8,128)(2,1)} async-done(((bf16[64,5,9,320]{3,1,2,0:T(8,128)(2,1)}), bf16[64,5,9,320]{3,1,2,0:T(8,128)(2,1)}, u32[]{:S(2)}, u32[]{:S(2)}) %all-to-all-start) | async-done | bytes 1843232 | tf_op jit(solution)/shard_map/all_to_all | solution.py:45
  191.4 4.3 copy.17
  195.7 5.5 %reshape.69 = bf16[320,9,320]{2,0,1:T(8,128)(2,1)} reshape(bf16[64,5,9,320]{3,1,0,2:T(8,128)(2,1)} %copy.17) | data formatting | bytes 3686400 | tf_op jit(solution)/shard_map/reshape | solution.py:44
  201.2 0.0 copy-start.2
  201.2 1.5 fusion.32
  202.7 1.4 fusion.31
  204.2 0.0 copy-done.2
  204.2 0.4 convolution_add_fusion.6
  204.6 0.4 convolution_add_fusion.5
  205.0 0.5 convolution_add_fusion.4
  205.5 0.4 convolution_add_fusion.3
  206.0 0.4 convolution_add_fusion.2
  206.4 0.5 convolution_add_fusion.1
  206.9 1.2 fusion.8
  208.1 159.5 %reduce-scatter.3.cloned.1.call-done = f32[5,9,320]{2,1,0:T(8,128)} async-done(((f32[320,9,320]{2,1,0:T(8,128)}), f32[5,9,320]{2,1,0:T(8,128)}) %reduce-scatter.3.cloned.1.call-update) | async-done | bytes 57616 | tf_op jit(solution)/shard_map/reduce_scatter | solution.py:63
  367.5 54.7 %all-reduce.1 = f32[5,9,320]{2,1,0:T(8,128)S(1)} all-reduce(f32[5,9,320]{2,1,0:T(8,128)} %reduce-scatter.3.cloned.1.call-done), channel_id=3, replica_groups=mesh['band'=64,'strip'=8] {'strip'}, use_global_device_ids=true, to_apply=%region_1.2.clone | all-reduce | flops 14400 | bytes 115200
  422.2 0.1 dynamic-slice_multiply_fusion
  422.3 0.6 copy.20
Async XLA Ops:
  7.2 10.7 %copy-start = (bf16[1,320,6,128]{3,1,2,0:T(8,128)(2,1)S(1)}, bf16[1,320,6,128]{3,1,2,0:T(8,128)(2,1)}, u32[]{:S(2)}) copy-start(bf16[1,320,6,128]{3,1,2,0:T(8,128)(2,1)} %param.3) | copy-start | bytes 1474564
  7.2 12.0 %copy-start.1 = (bf16[1,320,6,128]{3,1,2,0:T(8,128)(2,1)S(1)}, bf16[1,320,6,128]{3,1,2,0:T(8,128)(2,1)}, u32[]{:S(2)}) copy-start(bf16[1,320,6,128]{3,1,2,0:T(8,128)(2,1)} %param.4) | copy-start | bytes 1474564
  7.2 360.4 %reduce-scatter.3.cloned.1.call-start = ((), (), s32[]{:S(2)}) async-start(), calls=%async_computation.2 | async-start | bytes 7987200 | tf_op jit(solution)/shard_map/reduce_scatter | solution.py:63
  8.3 6.3 %collective-permute-start.1 = (bf16[1,320,1,128]{3,1,2,0:T(8,128)(2,1)S(1)}, bf16[1,320,1,128]{3,1,2,0:T(8,128)(2,1)S(1)}, u32[]{:S(2)}, u32[]{:S(2)}) collective-permute-start(bf16[1,320,1,128]{3,1,2,0:T(8,128)(2,1)S(1)} %get-tuple-element.11), channel_id=1, source_target_pairs={{1,0},{2,1},{3,2},{4,3},{5,4},{6,5},{7,6},{9,8},{10,9},{11,10},{12... | collective-permute-start | bytes 245768 | tf_op jit(solution)/shard_map/ppermute | solution.py:20
  9.6 6.6 %collective-permute-start = (bf16[1,320,1,128]{3,1,2,0:T(8,128)(2,1)S(1)}, bf16[1,320,1,128]{3,1,2,0:T(8,128)(2,1)S(1)}, u32[]{:S(2)}, u32[]{:S(2)}) collective-permute-start(bf16[1,320,1,128]{3,1,2,0:T(8,128)(2,1)S(1)} %get-tuple-element.10), channel_id=1, source_target_pairs={{0,1},{1,2},{2,3},{3,4},{4,5},{5,6},{6,7},{8,9},{9,10},{10,11},{11... | collective-permute-start | bytes 245768 | tf_op jit(solution)/shard_map/ppermute | solution.py:18
  38.1 0.7 copy-start.3
  88.8 102.6 %all-to-all-start = ((bf16[64,5,9,320]{3,1,2,0:T(8,128)(2,1)}), bf16[64,5,9,320]{3,1,2,0:T(8,128)(2,1)}, u32[]{:S(2)}, u32[]{:S(2)}) async-start(bf16[64,5,9,320]{3,1,2,0:T(8,128)(2,1)} %stack.22), calls=%async_computation | async-start | bytes 7077888 | tf_op jit(solution)/shard_map/all_to_all | solution.py:45
  201.2 3.0 copy-start.2
Sparse Core Ops, SparseCore 0:
  38.3 329.2 reduce-scatter.2
